TPU v7x, 256 devices: a whole 4x4x8 slice. The times are simulated.
256 devices in a mesh: seq: 32 (over y, x, core), head: 8 (over z).
Axes of the slice: x: 4, y: 4, z: 8, core: 2. Of those that a mesh axis runs over, the one named last changes fastest.
Arguments:
- queries: bfloat16 [32768, 8192], P(('seq', 'head')), may hold values from -6 to 6
- key_vectors: bfloat16 [32768, 8192], P(('seq', 'head')), may hold values from -6 to 6
- value_vectors: bfloat16 [32768, 8192], P(('seq', 'head')), may hold values from -6 to 6
- out_gain: float32 [64, 128], P('head'), may hold values from 0.1 to 1.9
Outputs:
- attended: bfloat16 [32768, 8192], P(('seq', 'head'))
All inputs are finite; a program needn't handle non-finite values.
Results may differ from a plain program's by a relative error of at most 0.0049.
Values may be sent and summed in bfloat16 or wider, within the bound.
A program may use at most 128 MiB of HBM per device.

v0:
```python
import jax
import jax.numpy as jnp
from jax import lax
from jax.sharding import PartitionSpec as P

HEADS = 64
HD = 128
BLOCK = 512


def passed_along(block, axis, distance):
    devices = range(lax.axis_size(axis))
    route = [(i - distance, i) for i in devices if i - distance in devices]
    return lax.ppermute(block, axis, route)


def split_heads(matrix):
    return matrix.reshape(matrix.shape[0], HEADS, HD)


def to_blocks(tensor):
    return tensor.reshape(tensor.shape[0] // BLOCK, BLOCK, tensor.shape[1], HD)


def block_states(key_heads, value_heads):
    return jnp.einsum(
        "nbhd,nbhe->nhde",
        to_blocks(key_heads),
        to_blocks(value_heads),
        preferred_element_type=jnp.float32,
    )


def carried_states(states):
    own = jnp.sum(states, axis=0)
    seq_count = lax.axis_size("seq")

    def relay(step, prefix):
        return passed_along(prefix + own, "seq", 1)

    prefix = lax.fori_loop(0, seq_count - 1, relay, jnp.zeros_like(own))
    carried = prefix[None] + (jnp.cumsum(states, axis=0) - states)
    return carried.astype(jnp.bfloat16)


def per_device(queries, key_vectors, value_vectors, out_gain):
    query_heads, key_heads, value_heads = (
        lax.all_to_all(split_heads(queries), "head", split_axis=1, concat_axis=0, tiled=True),
        lax.all_to_all(split_heads(key_vectors), "head", split_axis=1, concat_axis=0, tiled=True),
        lax.all_to_all(split_heads(value_vectors), "head", split_axis=1, concat_axis=0, tiled=True),
    )
    carried = carried_states(block_states(key_heads, value_heads))
    query_blocks = to_blocks(query_heads)
    key_blocks = to_blocks(key_heads)
    value_blocks = to_blocks(value_heads)
    inter = jnp.einsum("nbhd,nhde->nbhe", query_blocks, carried, preferred_element_type=jnp.float32)
    scores = jnp.einsum(
        "nbhd,nchd->nhbc", query_blocks, key_blocks, preferred_element_type=jnp.float32
    )
    causal = jnp.arange(BLOCK)[:, None] >= jnp.arange(BLOCK)[None, :]
    scores = jnp.where(causal[None, None], scores, jnp.float32(0.0)).astype(jnp.bfloat16)
    intra = jnp.einsum("nhbc,nchd->nbhd", scores, value_blocks, preferred_element_type=jnp.float32)
    raw = inter + intra
    scale = lax.rsqrt(jnp.mean(raw * raw, axis=-1, keepdims=True) + 1e-06)
    normed = (raw * scale * out_gain[None, None]).astype(jnp.bfloat16)
    normed = normed.reshape(query_heads.shape[0], query_heads.shape[1], HD)
    tokens_back = lax.all_to_all(normed, "head", split_axis=0, concat_axis=1, tiled=True)
    return tokens_back.reshape(tokens_back.shape[0], HEADS * HD)


def solution(mesh):
    return jax.shard_map(
        per_device,
        mesh=mesh,
        in_specs=(
            P(("seq", "head"), None),
            P(("seq", "head"), None),
            P(("seq", "head"), None),
            P("head", None),
        ),
        out_specs=P(("seq", "head"), None),
        check_vma=False,
    )
```

profile of v0, /device:TPU:16, one launch (start us, length us, event | category | flops | bytes accessed | tf_op | source)
XLA Modules:
  0.0 646.3 jit_solution(1137800084721814047)
XLA Ops:
  22.7 43.1 %all-to-all-done = bf16[128,64,128]{2,0,1:T(8,128)(2,1)S(1)} async-done(((bf16[128,64,128]{2,0,1:T(8,128)(2,1)}), bf16[128,64,128]{2,0,1:T(8,128)(2,1)S(1)}, u32[]{:S(2)}, u32[]{:S(2)}) %all-to-all-start) | async-done | bytes 2097184 | tf_op jit(solution)/shard_map/all_to_all | solution.py:49
  78.3 43.5 %all-to-all-done.1 = bf16[128,64,128]{2,0,1:T(8,128)(2,1)} async-done(((bf16[128,64,128]{2,0,1:T(8,128)(2,1)}), bf16[128,64,128]{2,0,1:T(8,128)(2,1)}, u32[]{:S(2)}, u32[]{:S(2)}) %all-to-all-start.1) | async-done | bytes 2097184 | tf_op jit(solution)/shard_map/all_to_all | solution.py:50
  132.0 43.0 %all-to-all-done.2 = bf16[128,64,128]{2,0,1:T(8,128)(2,1)} async-done(((bf16[128,64,128]{2,0,1:T(8,128)(2,1)}), bf16[128,64,128]{2,0,1:T(8,128)(2,1)}, u32[]{:S(2)}, u32[]{:S(2)}) %all-to-all-start.2) | async-done | bytes 2097184 | tf_op jit(solution)/shard_map/all_to_all | solution.py:48
  181.6 392.8 %while.10 = (s32[]{:T(128)}, f32[8,128,128]{2,1,0:T(8,128)S(1)}, f32[8,128,128]{2,1,0:T(8,128)S(1)}, s32[]{:T(128)}) while((s32[]{:T(128)}, f32[8,128,128]{2,1,0:T(8,128)S(1)}, f32[8,128,128]{2,1,0:T(8,128)S(1)}, s32[]{:T(128)}) %tuple.20), condition=%wide.region_2.0_spmd, body=%wide.region_1.0_spmd.sunk | while | flops 131074 | bytes 3670109 | solution.py:41
  183.6 10.7 %collective-permute-done = f32[8,128,128]{2,1,0:T(8,128)S(1)} collective-permute-done((f32[8,128,128]{2,1,0:T(8,128)S(1)}, f32[8,128,128]{2,1,0:T(8,128)S(1)}, u32[]{:S(2)}, u32[]{:S(2)}) %collective-permute-start) | collective-permute-done | bytes 524320 | tf_op jit(solution)/shard_map/while/body/eval_jaxpr/ppermute | solution.py:14
  196.3 10.7 %collective-permute-done = f32[8,128,128]{2,1,0:T(8,128)S(1)} collective-permute-done((f32[8,128,128]{2,1,0:T(8,128)S(1)}, f32[8,128,128]{2,1,0:T(8,128)S(1)}, u32[]{:S(2)}, u32[]{:S(2)}) %collective-permute-start) | collective-permute-done | bytes 524320 | tf_op jit(solution)/shard_map/while/body/eval_jaxpr/ppermute | solution.py:14
  209.0 10.7 %collective-permute-done = f32[8,128,128]{2,1,0:T(8,128)S(1)} collective-permute-done((f32[8,128,128]{2,1,0:T(8,128)S(1)}, f32[8,128,128]{2,1,0:T(8,128)S(1)}, u32[]{:S(2)}, u32[]{:S(2)}) %collective-permute-start) | collective-permute-done | bytes 524320 | tf_op jit(solution)/shard_map/while/body/eval_jaxpr/ppermute | solution.py:14
  221.6 10.7 %collective-permute-done = f32[8,128,128]{2,1,0:T(8,128)S(1)} collective-permute-done((f32[8,128,128]{2,1,0:T(8,128)S(1)}, f32[8,128,128]{2,1,0:T(8,128)S(1)}, u32[]{:S(2)}, u32[]{:S(2)}) %collective-permute-start) | collective-permute-done | bytes 524320 | tf_op jit(solution)/shard_map/while/body/eval_jaxpr/ppermute | solution.py:14
  234.3 10.7 %collective-permute-done = f32[8,128,128]{2,1,0:T(8,128)S(1)} collective-permute-done((f32[8,128,128]{2,1,0:T(8,128)S(1)}, f32[8,128,128]{2,1,0:T(8,128)S(1)}, u32[]{:S(2)}, u32[]{:S(2)}) %collective-permute-start) | collective-permute-done | bytes 524320 | tf_op jit(solution)/shard_map/while/body/eval_jaxpr/ppermute | solution.py:14
  247.0 10.7 %collective-permute-done = f32[8,128,128]{2,1,0:T(8,128)S(1)} collective-permute-done((f32[8,128,128]{2,1,0:T(8,128)S(1)}, f32[8,128,128]{2,1,0:T(8,128)S(1)}, u32[]{:S(2)}, u32[]{:S(2)}) %collective-permute-start) | collective-permute-done | bytes 524320 | tf_op jit(solution)/shard_map/while/body/eval_jaxpr/ppermute | solution.py:14
  259.7 10.7 %collective-permute-done = f32[8,128,128]{2,1,0:T(8,128)S(1)} collective-permute-done((f32[8,128,128]{2,1,0:T(8,128)S(1)}, f32[8,128,128]{2,1,0:T(8,128)S(1)}, u32[]{:S(2)}, u32[]{:S(2)}) %collective-permute-start) | collective-permute-done | bytes 524320 | tf_op jit(solution)/shard_map/while/body/eval_jaxpr/ppermute | solution.py:14
  272.3 10.7 %collective-permute-done = f32[8,128,128]{2,1,0:T(8,128)S(1)} collective-permute-done((f32[8,128,128]{2,1,0:T(8,128)S(1)}, f32[8,128,128]{2,1,0:T(8,128)S(1)}, u32[]{:S(2)}, u32[]{:S(2)}) %collective-permute-start) | collective-permute-done | bytes 524320 | tf_op jit(solution)/shard_map/while/body/eval_jaxpr/ppermute | solution.py:14
  285.0 10.7 %collective-permute-done = f32[8,128,128]{2,1,0:T(8,128)S(1)} collective-permute-done((f32[8,128,128]{2,1,0:T(8,128)S(1)}, f32[8,128,128]{2,1,0:T(8,128)S(1)}, u32[]{:S(2)}, u32[]{:S(2)}) %collective-permute-start) | collective-permute-done | bytes 524320 | tf_op jit(solution)/shard_map/while/body/eval_jaxpr/ppermute | solution.py:14
  297.7 10.7 %collective-permute-done = f32[8,128,128]{2,1,0:T(8,128)S(1)} collective-permute-done((f32[8,128,128]{2,1,0:T(8,128)S(1)}, f32[8,128,128]{2,1,0:T(8,128)S(1)}, u32[]{:S(2)}, u32[]{:S(2)}) %collective-permute-start) | collective-permute-done | bytes 524320 | tf_op jit(solution)/shard_map/while/body/eval_jaxpr/ppermute | solution.py:14
  310.3 10.7 %collective-permute-done = f32[8,128,128]{2,1,0:T(8,128)S(1)} collective-permute-done((f32[8,128,128]{2,1,0:T(8,128)S(1)}, f32[8,128,128]{2,1,0:T(8,128)S(1)}, u32[]{:S(2)}, u32[]{:S(2)}) %collective-permute-start) | collective-permute-done | bytes 524320 | tf_op jit(solution)/shard_map/while/body/eval_jaxpr/ppermute | solution.py:14
  323.0 10.7 %collective-permute-done = f32[8,128,128]{2,1,0:T(8,128)S(1)} collective-permute-done((f32[8,128,128]{2,1,0:T(8,128)S(1)}, f32[8,128,128]{2,1,0:T(8,128)S(1)}, u32[]{:S(2)}, u32[]{:S(2)}) %collective-permute-start) | collective-permute-done | bytes 524320 | tf_op jit(solution)/shard_map/while/body/eval_jaxpr/ppermute | solution.py:14
  335.7 10.7 %collective-permute-done = f32[8,128,128]{2,1,0:T(8,128)S(1)} collective-permute-done((f32[8,128,128]{2,1,0:T(8,128)S(1)}, f32[8,128,128]{2,1,0:T(8,128)S(1)}, u32[]{:S(2)}, u32[]{:S(2)}) %collective-permute-start) | collective-permute-done | bytes 524320 | tf_op jit(solution)/shard_map/while/body/eval_jaxpr/ppermute | solution.py:14
  348.3 10.7 %collective-permute-done = f32[8,128,128]{2,1,0:T(8,128)S(1)} collective-permute-done((f32[8,128,128]{2,1,0:T(8,128)S(1)}, f32[8,128,128]{2,1,0:T(8,128)S(1)}, u32[]{:S(2)}, u32[]{:S(2)}) %collective-permute-start) | collective-permute-done | bytes 524320 | tf_op jit(solution)/shard_map/while/body/eval_jaxpr/ppermute | solution.py:14
  361.0 10.7 %collective-permute-done = f32[8,128,128]{2,1,0:T(8,128)S(1)} collective-permute-done((f32[8,128,128]{2,1,0:T(8,128)S(1)}, f32[8,128,128]{2,1,0:T(8,128)S(1)}, u32[]{:S(2)}, u32[]{:S(2)}) %collective-permute-start) | collective-permute-done | bytes 524320 | tf_op jit(solution)/shard_map/while/body/eval_jaxpr/ppermute | solution.py:14
  373.7 10.7 %collective-permute-done = f32[8,128,128]{2,1,0:T(8,128)S(1)} collective-permute-done((f32[8,128,128]{2,1,0:T(8,128)S(1)}, f32[8,128,128]{2,1,0:T(8,128)S(1)}, u32[]{:S(2)}, u32[]{:S(2)}) %collective-permute-start) | collective-permute-done | bytes 524320 | tf_op jit(solution)/shard_map/while/body/eval_jaxpr/ppermute | solution.py:14
  386.4 10.7 %collective-permute-done = f32[8,128,128]{2,1,0:T(8,128)S(1)} collective-permute-done((f32[8,128,128]{2,1,0:T(8,128)S(1)}, f32[8,128,128]{2,1,0:T(8,128)S(1)}, u32[]{:S(2)}, u32[]{:S(2)}) %collective-permute-start) | collective-permute-done | bytes 524320 | tf_op jit(solution)/shard_map/while/body/eval_jaxpr/ppermute | solution.py:14
  399.0 10.7 %collective-permute-done = f32[8,128,128]{2,1,0:T(8,128)S(1)} collective-permute-done((f32[8,128,128]{2,1,0:T(8,128)S(1)}, f32[8,128,128]{2,1,0:T(8,128)S(1)}, u32[]{:S(2)}, u32[]{:S(2)}) %collective-permute-start) | collective-permute-done | bytes 524320 | tf_op jit(solution)/shard_map/while/body/eval_jaxpr/ppermute | solution.py:14
  411.7 10.7 %collective-permute-done = f32[8,128,128]{2,1,0:T(8,128)S(1)} collective-permute-done((f32[8,128,128]{2,1,0:T(8,128)S(1)}, f32[8,128,128]{2,1,0:T(8,128)S(1)}, u32[]{:S(2)}, u32[]{:S(2)}) %collective-permute-start) | collective-permute-done | bytes 524320 | tf_op jit(solution)/shard_map/while/body/eval_jaxpr/ppermute | solution.py:14
  424.4 10.7 %collective-permute-done = f32[8,128,128]{2,1,0:T(8,128)S(1)} collective-permute-done((f32[8,128,128]{2,1,0:T(8,128)S(1)}, f32[8,128,128]{2,1,0:T(8,128)S(1)}, u32[]{:S(2)}, u32[]{:S(2)}) %collective-permute-start) | collective-permute-done | bytes 524320 | tf_op jit(solution)/shard_map/while/body/eval_jaxpr/ppermute | solution.py:14
  437.0 10.7 %collective-permute-done = f32[8,128,128]{2,1,0:T(8,128)S(1)} collective-permute-done((f32[8,128,128]{2,1,0:T(8,128)S(1)}, f32[8,128,128]{2,1,0:T(8,128)S(1)}, u32[]{:S(2)}, u32[]{:S(2)}) %collective-permute-start) | collective-permute-done | bytes 524320 | tf_op jit(solution)/shard_map/while/body/eval_jaxpr/ppermute | solution.py:14
  449.7 10.7 %collective-permute-done = f32[8,128,128]{2,1,0:T(8,128)S(1)} collective-permute-done((f32[8,128,128]{2,1,0:T(8,128)S(1)}, f32[8,128,128]{2,1,0:T(8,128)S(1)}, u32[]{:S(2)}, u32[]{:S(2)}) %collective-permute-start) | collective-permute-done | bytes 524320 | tf_op jit(solution)/shard_map/while/body/eval_jaxpr/ppermute | solution.py:14
  462.4 10.7 %collective-permute-done = f32[8,128,128]{2,1,0:T(8,128)S(1)} collective-permute-done((f32[8,128,128]{2,1,0:T(8,128)S(1)}, f32[8,128,128]{2,1,0:T(8,128)S(1)}, u32[]{:S(2)}, u32[]{:S(2)}) %collective-permute-start) | collective-permute-done | bytes 524320 | tf_op jit(solution)/shard_map/while/body/eval_jaxpr/ppermute | solution.py:14
  475.0 10.7 %collective-permute-done = f32[8,128,128]{2,1,0:T(8,128)S(1)} collective-permute-done((f32[8,128,128]{2,1,0:T(8,128)S(1)}, f32[8,128,128]{2,1,0:T(8,128)S(1)}, u32[]{:S(2)}, u32[]{:S(2)}) %collective-permute-start) | collective-permute-done | bytes 524320 | tf_op jit(solution)/shard_map/while/body/eval_jaxpr/ppermute | solution.py:14
  487.7 10.7 %collective-permute-done = f32[8,128,128]{2,1,0:T(8,128)S(1)} collective-permute-done((f32[8,128,128]{2,1,0:T(8,128)S(1)}, f32[8,128,128]{2,1,0:T(8,128)S(1)}, u32[]{:S(2)}, u32[]{:S(2)}) %collective-permute-start) | collective-permute-done | bytes 524320 | tf_op jit(solution)/shard_map/while/body/eval_jaxpr/ppermute | solution.py:14
  500.4 10.7 %collective-permute-done = f32[8,128,128]{2,1,0:T(8,128)S(1)} collective-permute-done((f32[8,128,128]{2,1,0:T(8,128)S(1)}, f32[8,128,128]{2,1,0:T(8,128)S(1)}, u32[]{:S(2)}, u32[]{:S(2)}) %collective-permute-start) | collective-permute-done | bytes 524320 | tf_op jit(solution)/shard_map/while/body/eval_jaxpr/ppermute | solution.py:14
  513.1 10.7 %collective-permute-done = f32[8,128,128]{2,1,0:T(8,128)S(1)} collective-permute-done((f32[8,128,128]{2,1,0:T(8,128)S(1)}, f32[8,128,128]{2,1,0:T(8,128)S(1)}, u32[]{:S(2)}, u32[]{:S(2)}) %collective-permute-start) | collective-permute-done | bytes 524320 | tf_op jit(solution)/shard_map/while/body/eval_jaxpr/ppermute | solution.py:14
  594.1 46.0 %all_to_all.60 = bf16[1024,8,128]{2,1,0:T(8,128)(2,1)} all-to-all(bf16[1024,8,128]{2,1,0:T(8,128)(2,1)S(1)} %bitcast.27), channel_id=1, replica_groups=mesh['seq'=32,'head'=8] {'head'}, dimensions={0} | all-to-all | bytes 4194304 | tf_op jit(solution)/shard_map/all_to_all | solution.py:67
  (97 shorter events, 181.8 us)
Async XLA Ops:
  6.1 59.7 %all-to-all-start = ((bf16[128,64,128]{2,0,1:T(8,128)(2,1)}), bf16[128,64,128]{2,0,1:T(8,128)(2,1)S(1)}, u32[]{:S(2)}, u32[]{:S(2)}) async-start(bf16[128,64,128]{2,0,1:T(8,128)(2,1)} %copy.46), calls=%async_computation | async-start | bytes 4194304 | tf_op jit(solution)/shard_map/all_to_all | solution.py:49
  65.8 56.0 %all-to-all-start.1 = ((bf16[128,64,128]{2,0,1:T(8,128)(2,1)}), bf16[128,64,128]{2,0,1:T(8,128)(2,1)}, u32[]{:S(2)}, u32[]{:S(2)}) async-start(bf16[128,64,128]{2,0,1:T(8,128)(2,1)} %copy.50), calls=%async_computation.1 | async-start | bytes 4194304 | tf_op jit(solution)/shard_map/all_to_all | solution.py:50
  121.8 53.2 %all-to-all-start.2 = ((bf16[128,64,128]{2,0,1:T(8,128)(2,1)}), bf16[128,64,128]{2,0,1:T(8,128)(2,1)}, u32[]{:S(2)}, u32[]{:S(2)}) async-start(bf16[128,64,128]{2,0,1:T(8,128)(2,1)} %copy.56), calls=%async_computation.2 | async-start | bytes 4194304 | tf_op jit(solution)/shard_map/all_to_all | solution.py:48
  181.7 12.6 %collective-permute-start = (f32[8,128,128]{2,1,0:T(8,128)S(1)}, f32[8,128,128]{2,1,0:T(8,128)S(1)}, u32[]{:S(2)}, u32[]{:S(2)}) collective-permute-start(f32[8,128,128]{2,1,0:T(8,128)S(1)} %add.43), channel_id=1, source_target_pairs={{0,8},{8,16},{16,24},{24,32},{32,40},{40,48},{48,56},{56,64},{64,7... | collective-permute-start | bytes 1572872 | tf_op jit(solution)/shard_map/while/body/eval_jaxpr/ppermute | solution.py:14
  194.4 12.6 %collective-permute-start = (f32[8,128,128]{2,1,0:T(8,128)S(1)}, f32[8,128,128]{2,1,0:T(8,128)S(1)}, u32[]{:S(2)}, u32[]{:S(2)}) collective-permute-start(f32[8,128,128]{2,1,0:T(8,128)S(1)} %add.43), channel_id=1, source_target_pairs={{0,8},{8,16},{16,24},{24,32},{32,40},{40,48},{48,56},{56,64},{64,7... | collective-permute-start | bytes 1572872 | tf_op jit(solution)/shard_map/while/body/eval_jaxpr/ppermute | solution.py:14
  207.0 12.6 %collective-permute-start = (f32[8,128,128]{2,1,0:T(8,128)S(1)}, f32[8,128,128]{2,1,0:T(8,128)S(1)}, u32[]{:S(2)}, u32[]{:S(2)}) collective-permute-start(f32[8,128,128]{2,1,0:T(8,128)S(1)} %add.43), channel_id=1, source_target_pairs={{0,8},{8,16},{16,24},{24,32},{32,40},{40,48},{48,56},{56,64},{64,7... | collective-permute-start | bytes 1572872 | tf_op jit(solution)/shard_map/while/body/eval_jaxpr/ppermute | solution.py:14
  219.7 12.6 %collective-permute-start = (f32[8,128,128]{2,1,0:T(8,128)S(1)}, f32[8,128,128]{2,1,0:T(8,128)S(1)}, u32[]{:S(2)}, u32[]{:S(2)}) collective-permute-start(f32[8,128,128]{2,1,0:T(8,128)S(1)} %add.43), channel_id=1, source_target_pairs={{0,8},{8,16},{16,24},{24,32},{32,40},{40,48},{48,56},{56,64},{64,7... | collective-permute-start | bytes 1572872 | tf_op jit(solution)/shard_map/while/body/eval_jaxpr/ppermute | solution.py:14
  232.4 12.6 %collective-permute-start = (f32[8,128,128]{2,1,0:T(8,128)S(1)}, f32[8,128,128]{2,1,0:T(8,128)S(1)}, u32[]{:S(2)}, u32[]{:S(2)}) collective-permute-start(f32[8,128,128]{2,1,0:T(8,128)S(1)} %add.43), channel_id=1, source_target_pairs={{0,8},{8,16},{16,24},{24,32},{32,40},{40,48},{48,56},{56,64},{64,7... | collective-permute-start | bytes 1572872 | tf_op jit(solution)/shard_map/while/body/eval_jaxpr/ppermute | solution.py:14
  245.1 12.6 %collective-permute-start = (f32[8,128,128]{2,1,0:T(8,128)S(1)}, f32[8,128,128]{2,1,0:T(8,128)S(1)}, u32[]{:S(2)}, u32[]{:S(2)}) collective-permute-start(f32[8,128,128]{2,1,0:T(8,128)S(1)} %add.43), channel_id=1, source_target_pairs={{0,8},{8,16},{16,24},{24,32},{32,40},{40,48},{48,56},{56,64},{64,7... | collective-permute-start | bytes 1572872 | tf_op jit(solution)/shard_map/while/body/eval_jaxpr/ppermute | solution.py:14
  257.7 12.6 %collective-permute-start = (f32[8,128,128]{2,1,0:T(8,128)S(1)}, f32[8,128,128]{2,1,0:T(8,128)S(1)}, u32[]{:S(2)}, u32[]{:S(2)}) collective-permute-start(f32[8,128,128]{2,1,0:T(8,128)S(1)} %add.43), channel_id=1, source_target_pairs={{0,8},{8,16},{16,24},{24,32},{32,40},{40,48},{48,56},{56,64},{64,7... | collective-permute-start | bytes 1572872 | tf_op jit(solution)/shard_map/while/body/eval_jaxpr/ppermute | solution.py:14
  270.4 12.6 %collective-permute-start = (f32[8,128,128]{2,1,0:T(8,128)S(1)}, f32[8,128,128]{2,1,0:T(8,128)S(1)}, u32[]{:S(2)}, u32[]{:S(2)}) collective-permute-start(f32[8,128,128]{2,1,0:T(8,128)S(1)} %add.43), channel_id=1, source_target_pairs={{0,8},{8,16},{16,24},{24,32},{32,40},{40,48},{48,56},{56,64},{64,7... | collective-permute-start | bytes 1572872 | tf_op jit(solution)/shard_map/while/body/eval_jaxpr/ppermute | solution.py:14
  283.1 12.6 %collective-permute-start = (f32[8,128,128]{2,1,0:T(8,128)S(1)}, f32[8,128,128]{2,1,0:T(8,128)S(1)}, u32[]{:S(2)}, u32[]{:S(2)}) collective-permute-start(f32[8,128,128]{2,1,0:T(8,128)S(1)} %add.43), channel_id=1, source_target_pairs={{0,8},{8,16},{16,24},{24,32},{32,40},{40,48},{48,56},{56,64},{64,7... | collective-permute-start | bytes 1572872 | tf_op jit(solution)/shard_map/while/body/eval_jaxpr/ppermute | solution.py:14
  295.7 12.6 %collective-permute-start = (f32[8,128,128]{2,1,0:T(8,128)S(1)}, f32[8,128,128]{2,1,0:T(8,128)S(1)}, u32[]{:S(2)}, u32[]{:S(2)}) collective-permute-start(f32[8,128,128]{2,1,0:T(8,128)S(1)} %add.43), channel_id=1, source_target_pairs={{0,8},{8,16},{16,24},{24,32},{32,40},{40,48},{48,56},{56,64},{64,7... | collective-permute-start | bytes 1572872 | tf_op jit(solution)/shard_map/while/body/eval_jaxpr/ppermute | solution.py:14
  308.4 12.6 %collective-permute-start = (f32[8,128,128]{2,1,0:T(8,128)S(1)}, f32[8,128,128]{2,1,0:T(8,128)S(1)}, u32[]{:S(2)}, u32[]{:S(2)}) collective-permute-start(f32[8,128,128]{2,1,0:T(8,128)S(1)} %add.43), channel_id=1, source_target_pairs={{0,8},{8,16},{16,24},{24,32},{32,40},{40,48},{48,56},{56,64},{64,7... | collective-permute-start | bytes 1572872 | tf_op jit(solution)/shard_map/while/body/eval_jaxpr/ppermute | solution.py:14
  321.1 12.6 %collective-permute-start = (f32[8,128,128]{2,1,0:T(8,128)S(1)}, f32[8,128,128]{2,1,0:T(8,128)S(1)}, u32[]{:S(2)}, u32[]{:S(2)}) collective-permute-start(f32[8,128,128]{2,1,0:T(8,128)S(1)} %add.43), channel_id=1, source_target_pairs={{0,8},{8,16},{16,24},{24,32},{32,40},{40,48},{48,56},{56,64},{64,7... | collective-permute-start | bytes 1572872 | tf_op jit(solution)/shard_map/while/body/eval_jaxpr/ppermute | solution.py:14
  333.7 12.6 %collective-permute-start = (f32[8,128,128]{2,1,0:T(8,128)S(1)}, f32[8,128,128]{2,1,0:T(8,128)S(1)}, u32[]{:S(2)}, u32[]{:S(2)}) collective-permute-start(f32[8,128,128]{2,1,0:T(8,128)S(1)} %add.43), channel_id=1, source_target_pairs={{0,8},{8,16},{16,24},{24,32},{32,40},{40,48},{48,56},{56,64},{64,7... | collective-permute-start | bytes 1572872 | tf_op jit(solution)/shard_map/while/body/eval_jaxpr/ppermute | solution.py:14
  346.4 12.6 %collective-permute-start = (f32[8,128,128]{2,1,0:T(8,128)S(1)}, f32[8,128,128]{2,1,0:T(8,128)S(1)}, u32[]{:S(2)}, u32[]{:S(2)}) collective-permute-start(f32[8,128,128]{2,1,0:T(8,128)S(1)} %add.43), channel_id=1, source_target_pairs={{0,8},{8,16},{16,24},{24,32},{32,40},{40,48},{48,56},{56,64},{64,7... | collective-permute-start | bytes 1572872 | tf_op jit(solution)/shard_map/while/body/eval_jaxpr/ppermute | solution.py:14
  359.1 12.6 %collective-permute-start = (f32[8,128,128]{2,1,0:T(8,128)S(1)}, f32[8,128,128]{2,1,0:T(8,128)S(1)}, u32[]{:S(2)}, u32[]{:S(2)}) collective-permute-start(f32[8,128,128]{2,1,0:T(8,128)S(1)} %add.43), channel_id=1, source_target_pairs={{0,8},{8,16},{16,24},{24,32},{32,40},{40,48},{48,56},{56,64},{64,7... | collective-permute-start | bytes 1572872 | tf_op jit(solution)/shard_map/while/body/eval_jaxpr/ppermute | solution.py:14
  371.8 12.6 %collective-permute-start = (f32[8,128,128]{2,1,0:T(8,128)S(1)}, f32[8,128,128]{2,1,0:T(8,128)S(1)}, u32[]{:S(2)}, u32[]{:S(2)}) collective-permute-start(f32[8,128,128]{2,1,0:T(8,128)S(1)} %add.43), channel_id=1, source_target_pairs={{0,8},{8,16},{16,24},{24,32},{32,40},{40,48},{48,56},{56,64},{64,7... | collective-permute-start | bytes 1572872 | tf_op jit(solution)/shard_map/while/body/eval_jaxpr/ppermute | solution.py:14
  384.4 12.6 %collective-permute-start = (f32[8,128,128]{2,1,0:T(8,128)S(1)}, f32[8,128,128]{2,1,0:T(8,128)S(1)}, u32[]{:S(2)}, u32[]{:S(2)}) collective-permute-start(f32[8,128,128]{2,1,0:T(8,128)S(1)} %add.43), channel_id=1, source_target_pairs={{0,8},{8,16},{16,24},{24,32},{32,40},{40,48},{48,56},{56,64},{64,7... | collective-permute-start | bytes 1572872 | tf_op jit(solution)/shard_map/while/body/eval_jaxpr/ppermute | solution.py:14
  397.1 12.6 %collective-permute-start = (f32[8,128,128]{2,1,0:T(8,128)S(1)}, f32[8,128,128]{2,1,0:T(8,128)S(1)}, u32[]{:S(2)}, u32[]{:S(2)}) collective-permute-start(f32[8,128,128]{2,1,0:T(8,128)S(1)} %add.43), channel_id=1, source_target_pairs={{0,8},{8,16},{16,24},{24,32},{32,40},{40,48},{48,56},{56,64},{64,7... | collective-permute-start | bytes 1572872 | tf_op jit(solution)/shard_map/while/body/eval_jaxpr/ppermute | solution.py:14
  409.8 12.6 %collective-permute-start = (f32[8,128,128]{2,1,0:T(8,128)S(1)}, f32[8,128,128]{2,1,0:T(8,128)S(1)}, u32[]{:S(2)}, u32[]{:S(2)}) collective-permute-start(f32[8,128,128]{2,1,0:T(8,128)S(1)} %add.43), channel_id=1, source_target_pairs={{0,8},{8,16},{16,24},{24,32},{32,40},{40,48},{48,56},{56,64},{64,7... | collective-permute-start | bytes 1572872 | tf_op jit(solution)/shard_map/while/body/eval_jaxpr/ppermute | solution.py:14
  422.4 12.6 %collective-permute-start = (f32[8,128,128]{2,1,0:T(8,128)S(1)}, f32[8,128,128]{2,1,0:T(8,128)S(1)}, u32[]{:S(2)}, u32[]{:S(2)}) collective-permute-start(f32[8,128,128]{2,1,0:T(8,128)S(1)} %add.43), channel_id=1, source_target_pairs={{0,8},{8,16},{16,24},{24,32},{32,40},{40,48},{48,56},{56,64},{64,7... | collective-permute-start | bytes 1572872 | tf_op jit(solution)/shard_map/while/body/eval_jaxpr/ppermute | solution.py:14
  435.1 12.6 %collective-permute-start = (f32[8,128,128]{2,1,0:T(8,128)S(1)}, f32[8,128,128]{2,1,0:T(8,128)S(1)}, u32[]{:S(2)}, u32[]{:S(2)}) collective-permute-start(f32[8,128,128]{2,1,0:T(8,128)S(1)} %add.43), channel_id=1, source_target_pairs={{0,8},{8,16},{16,24},{24,32},{32,40},{40,48},{48,56},{56,64},{64,7... | collective-permute-start | bytes 1572872 | tf_op jit(solution)/shard_map/while/body/eval_jaxpr/ppermute | solution.py:14
  447.8 12.6 %collective-permute-start = (f32[8,128,128]{2,1,0:T(8,128)S(1)}, f32[8,128,128]{2,1,0:T(8,128)S(1)}, u32[]{:S(2)}, u32[]{:S(2)}) collective-permute-start(f32[8,128,128]{2,1,0:T(8,128)S(1)} %add.43), channel_id=1, source_target_pairs={{0,8},{8,16},{16,24},{24,32},{32,40},{40,48},{48,56},{56,64},{64,7... | collective-permute-start | bytes 1572872 | tf_op jit(solution)/shard_map/while/body/eval_jaxpr/ppermute | solution.py:14
  460.4 12.6 %collective-permute-start = (f32[8,128,128]{2,1,0:T(8,128)S(1)}, f32[8,128,128]{2,1,0:T(8,128)S(1)}, u32[]{:S(2)}, u32[]{:S(2)}) collective-permute-start(f32[8,128,128]{2,1,0:T(8,128)S(1)} %add.43), channel_id=1, source_target_pairs={{0,8},{8,16},{16,24},{24,32},{32,40},{40,48},{48,56},{56,64},{64,7... | collective-permute-start | bytes 1572872 | tf_op jit(solution)/shard_map/while/body/eval_jaxpr/ppermute | solution.py:14
  473.1 12.6 %collective-permute-start = (f32[8,128,128]{2,1,0:T(8,128)S(1)}, f32[8,128,128]{2,1,0:T(8,128)S(1)}, u32[]{:S(2)}, u32[]{:S(2)}) collective-permute-start(f32[8,128,128]{2,1,0:T(8,128)S(1)} %add.43), channel_id=1, source_target_pairs={{0,8},{8,16},{16,24},{24,32},{32,40},{40,48},{48,56},{56,64},{64,7... | collective-permute-start | bytes 1572872 | tf_op jit(solution)/shard_map/while/body/eval_jaxpr/ppermute | solution.py:14
  485.8 12.6 %collective-permute-start = (f32[8,128,128]{2,1,0:T(8,128)S(1)}, f32[8,128,128]{2,1,0:T(8,128)S(1)}, u32[]{:S(2)}, u32[]{:S(2)}) collective-permute-start(f32[8,128,128]{2,1,0:T(8,128)S(1)} %add.43), channel_id=1, source_target_pairs={{0,8},{8,16},{16,24},{24,32},{32,40},{40,48},{48,56},{56,64},{64,7... | collective-permute-start | bytes 1572872 | tf_op jit(solution)/shard_map/while/body/eval_jaxpr/ppermute | solution.py:14
  498.5 12.6 %collective-permute-start = (f32[8,128,128]{2,1,0:T(8,128)S(1)}, f32[8,128,128]{2,1,0:T(8,128)S(1)}, u32[]{:S(2)}, u32[]{:S(2)}) collective-permute-start(f32[8,128,128]{2,1,0:T(8,128)S(1)} %add.43), channel_id=1, source_target_pairs={{0,8},{8,16},{16,24},{24,32},{32,40},{40,48},{48,56},{56,64},{64,7... | collective-permute-start | bytes 1572872 | tf_op jit(solution)/shard_map/while/body/eval_jaxpr/ppermute | solution.py:14
  511.1 12.6 %collective-permute-start = (f32[8,128,128]{2,1,0:T(8,128)S(1)}, f32[8,128,128]{2,1,0:T(8,128)S(1)}, u32[]{:S(2)}, u32[]{:S(2)}) collective-permute-start(f32[8,128,128]{2,1,0:T(8,128)S(1)} %add.43), channel_id=1, source_target_pairs={{0,8},{8,16},{16,24},{24,32},{32,40},{40,48},{48,56},{56,64},{64,7... | collective-permute-start | bytes 1572872 | tf_op jit(solution)/shard_map/while/body/eval_jaxpr/ppermute | solution.py:14
  523.8 12.6 %collective-permute-start = (f32[8,128,128]{2,1,0:T(8,128)S(1)}, f32[8,128,128]{2,1,0:T(8,128)S(1)}, u32[]{:S(2)}, u32[]{:S(2)}) collective-permute-start(f32[8,128,128]{2,1,0:T(8,128)S(1)} %add.43), channel_id=1, source_target_pairs={{0,8},{8,16},{16,24},{24,32},{32,40},{40,48},{48,56},{56,64},{64,7... | collective-permute-start | bytes 1572872 | tf_op jit(solution)/shard_map/while/body/eval_jaxpr/ppermute | solution.py:14
  536.5 12.6 %collective-permute-start = (f32[8,128,128]{2,1,0:T(8,128)S(1)}, f32[8,128,128]{2,1,0:T(8,128)S(1)}, u32[]{:S(2)}, u32[]{:S(2)}) collective-permute-start(f32[8,128,128]{2,1,0:T(8,128)S(1)} %add.43), channel_id=1, source_target_pairs={{0,8},{8,16},{16,24},{24,32},{32,40},{40,48},{48,56},{56,64},{64,7... | collective-permute-start | bytes 1572872 | tf_op jit(solution)/shard_map/while/body/eval_jaxpr/ppermute | solution.py:14
  (6 other events, 82.7 us)
where the time goes:
time: 648 us; the launch traced here: 646 us
  waiting for transfers between devices  461 us (71%)
  starting transfers between devices  76.7 us (12%)
  blocking collectives  46 us (7%)
  local copies, waits for them, and re-layouts  42.2 us (7%)
  matrix products  14.6 us (2%)
    ppermute x31, waiting for transfers between devices, passed_along(): return lax.ppermute(block, axis, route)  331 us
    ppermute x31, starting transfers between devices, passed_along(): return lax.ppermute(block, axis, route)  59.5 us
    all_to_all x1, blocking collectives, per_device(): lax.all_to_all(normed, 'head', split_axis=0, concat_axis=1, tiled=True)  46 us
    all_to_all x1, waiting for transfers between devices, per_device(): lax.all_to_all(split_heads(value_vectors), 'head', split_axis=1, concat_a...  43.5 us
    all_to_all x1, waiting for transfers between devices, per_device(): lax.all_to_all(split_heads(key_vectors), 'head', split_axis=1, concat_axi...  43.1 us
    all_to_all x1, waiting for transfers between devices, per_device(): lax.all_to_all(split_heads(queries), 'head', split_axis=1, concat_axis=0,...  43 us
  transfers between devices with their start and end apart: 34, of which 34 were waited for; matrix products, arithmetic and copies ran while one was open for 3% of the time, Pallas kernels for 0%

commit v1 on v0

--- a/solution.py
+++ b/solution.py
@@ -47,7 +47,15 @@
     query_heads, key_heads, value_heads = (
         lax.all_to_all(split_heads(queries), "head", split_axis=1, concat_axis=0, tiled=True),
         lax.all_to_all(split_heads(key_vectors), "head", split_axis=1, concat_axis=0, tiled=True),
-        lax.all_to_all(split_heads(value_vectors), "head", split_axis=1, concat_axis=0, tiled=True),
+        jnp.concatenate(
+            lax.all_to_all(
+                jnp.stack(jnp.split(split_heads(value_vectors), lax.axis_size("head"), 1)),
+                axis_name="head",
+                split_axis=0,
+                concat_axis=0,
+            ),
+            0,
+        ),
     )
     carried = carried_states(block_states(key_heads, value_heads))
     query_blocks = to_blocks(query_heads)

time: 648 us -> 611 us (0.943)
  waiting for transfers between devices: 461 us -> 418 us
    all_to_all x1, waiting for transfers between devices: 43 us -> 0.01 us  [per_device(): lax.all_to_all(split_heads(queries), 'head', split_axis=1, concat_axis=0,...]
    unnamed x11 -> x22, local copies, waits for them, and re-layouts: 11.7 us -> 17.1 us
  transfers between devices with their start and end apart: 34 -> 34, of which waited for: 34 -> 33; matrix products, arithmetic and copies ran while one was open for 3% -> 4% of each run, Pallas kernels for 0% -> 0%
where the time goes in v1:
time: 611 us; the launch traced here: 609 us
  waiting for transfers between devices  418 us (68%)
  starting transfers between devices  76.9 us (13%)
  blocking collectives  49.4 us (8%)
  local copies, waits for them, and re-layouts  46.6 us (8%)
  matrix products  13.8 us (2%)
    ppermute x31, waiting for transfers between devices, passed_along(): return lax.ppermute(block, axis, route)  331 us
    ppermute x31, starting transfers between devices, passed_along(): return lax.ppermute(block, axis, route)  59.5 us
    all_to_all x1, blocking collectives, per_device(): lax.all_to_all(normed, 'head', split_axis=0, concat_axis=1, tiled=True)  49.4 us
    all_to_all x1, waiting for transfers between devices, per_device(): lax.all_to_all(split_heads(key_vectors), 'head', split_axis=1, concat_axi...  43.5 us
    all_to_all x1, waiting for transfers between devices, per_device(): lax.all_to_all(jnp.stack(jnp.split(split_heads(value_vectors), lax.axis_s...  43.1 us
    unnamed x22, local copies, waits for them, and re-layouts  17.1 us
  transfers between devices with their start and end apart: 34, of which 33 were waited for; matrix products, arithmetic and copies ran while one was open for 4% of the time, Pallas kernels for 0%

profile of v1, /device:TPU:16, one launch (start us, length us, event | category | flops | bytes accessed | tf_op | source)
XLA Modules:
  0.0 609.5 jit_solution(1342917815631152329)
XLA Ops:
  25.0 43.1 %all-to-all-done = bf16[8,128,8,128]{3,2,1,0:T(8,128)(2,1)S(1)} async-done(((bf16[8,128,8,128]{3,2,1,0:T(8,128)(2,1)}), bf16[8,128,8,128]{3,2,1,0:T(8,128)(2,1)S(1)}, u32[]{:S(2)}, u32[]{:S(2)}) %all-to-all-start) | async-done | bytes 2097184 | tf_op jit(solution)/shard_map/all_to_all | solution.py:51
  80.5 43.5 %all-to-all-done.1 = bf16[128,64,128]{2,0,1:T(8,128)(2,1)} async-done(((bf16[128,64,128]{2,0,1:T(8,128)(2,1)}), bf16[128,64,128]{2,0,1:T(8,128)(2,1)}, u32[]{:S(2)}, u32[]{:S(2)}) %all-to-all-start.1) | async-done | bytes 2097184 | tf_op jit(solution)/shard_map/all_to_all | solution.py:49
  135.9 392.8 %while.10 = (s32[]{:T(128)}, f32[8,128,128]{2,1,0:T(8,128)S(1)}, f32[8,128,128]{2,1,0:T(8,128)S(1)}, s32[]{:T(128)}) while((s32[]{:T(128)}, f32[8,128,128]{2,1,0:T(8,128)S(1)}, f32[8,128,128]{2,1,0:T(8,128)S(1)}, s32[]{:T(128)}) %tuple.22), condition=%wide.region_2.0_spmd, body=%wide.region_1.0_spmd.sunk | while | flops 131074 | bytes 3670109 | solution.py:41
  137.9 10.7 %collective-permute-done = f32[8,128,128]{2,1,0:T(8,128)S(1)} collective-permute-done((f32[8,128,128]{2,1,0:T(8,128)S(1)}, f32[8,128,128]{2,1,0:T(8,128)S(1)}, u32[]{:S(2)}, u32[]{:S(2)}) %collective-permute-start) | collective-permute-done | bytes 524320 | tf_op jit(solution)/shard_map/while/body/eval_jaxpr/ppermute | solution.py:14
  150.6 10.7 %collective-permute-done = f32[8,128,128]{2,1,0:T(8,128)S(1)} collective-permute-done((f32[8,128,128]{2,1,0:T(8,128)S(1)}, f32[8,128,128]{2,1,0:T(8,128)S(1)}, u32[]{:S(2)}, u32[]{:S(2)}) %collective-permute-start) | collective-permute-done | bytes 524320 | tf_op jit(solution)/shard_map/while/body/eval_jaxpr/ppermute | solution.py:14
  163.3 10.7 %collective-permute-done = f32[8,128,128]{2,1,0:T(8,128)S(1)} collective-permute-done((f32[8,128,128]{2,1,0:T(8,128)S(1)}, f32[8,128,128]{2,1,0:T(8,128)S(1)}, u32[]{:S(2)}, u32[]{:S(2)}) %collective-permute-start) | collective-permute-done | bytes 524320 | tf_op jit(solution)/shard_map/while/body/eval_jaxpr/ppermute | solution.py:14
  175.9 10.7 %collective-permute-done = f32[8,128,128]{2,1,0:T(8,128)S(1)} collective-permute-done((f32[8,128,128]{2,1,0:T(8,128)S(1)}, f32[8,128,128]{2,1,0:T(8,128)S(1)}, u32[]{:S(2)}, u32[]{:S(2)}) %collective-permute-start) | collective-permute-done | bytes 524320 | tf_op jit(solution)/shard_map/while/body/eval_jaxpr/ppermute | solution.py:14
  188.6 10.7 %collective-permute-done = f32[8,128,128]{2,1,0:T(8,128)S(1)} collective-permute-done((f32[8,128,128]{2,1,0:T(8,128)S(1)}, f32[8,128,128]{2,1,0:T(8,128)S(1)}, u32[]{:S(2)}, u32[]{:S(2)}) %collective-permute-start) | collective-permute-done | bytes 524320 | tf_op jit(solution)/shard_map/while/body/eval_jaxpr/ppermute | solution.py:14
  201.3 10.7 %collective-permute-done = f32[8,128,128]{2,1,0:T(8,128)S(1)} collective-permute-done((f32[8,128,128]{2,1,0:T(8,128)S(1)}, f32[8,128,128]{2,1,0:T(8,128)S(1)}, u32[]{:S(2)}, u32[]{:S(2)}) %collective-permute-start) | collective-permute-done | bytes 524320 | tf_op jit(solution)/shard_map/while/body/eval_jaxpr/ppermute | solution.py:14
  214.0 10.7 %collective-permute-done = f32[8,128,128]{2,1,0:T(8,128)S(1)} collective-permute-done((f32[8,128,128]{2,1,0:T(8,128)S(1)}, f32[8,128,128]{2,1,0:T(8,128)S(1)}, u32[]{:S(2)}, u32[]{:S(2)}) %collective-permute-start) | collective-permute-done | bytes 524320 | tf_op jit(solution)/shard_map/while/body/eval_jaxpr/ppermute | solution.py:14
  226.6 10.7 %collective-permute-done = f32[8,128,128]{2,1,0:T(8,128)S(1)} collective-permute-done((f32[8,128,128]{2,1,0:T(8,128)S(1)}, f32[8,128,128]{2,1,0:T(8,128)S(1)}, u32[]{:S(2)}, u32[]{:S(2)}) %collective-permute-start) | collective-permute-done | bytes 524320 | tf_op jit(solution)/shard_map/while/body/eval_jaxpr/ppermute | solution.py:14
  239.3 10.7 %collective-permute-done = f32[8,128,128]{2,1,0:T(8,128)S(1)} collective-permute-done((f32[8,128,128]{2,1,0:T(8,128)S(1)}, f32[8,128,128]{2,1,0:T(8,128)S(1)}, u32[]{:S(2)}, u32[]{:S(2)}) %collective-permute-start) | collective-permute-done | bytes 524320 | tf_op jit(solution)/shard_map/while/body/eval_jaxpr/ppermute | solution.py:14
  252.0 10.7 %collective-permute-done = f32[8,128,128]{2,1,0:T(8,128)S(1)} collective-permute-done((f32[8,128,128]{2,1,0:T(8,128)S(1)}, f32[8,128,128]{2,1,0:T(8,128)S(1)}, u32[]{:S(2)}, u32[]{:S(2)}) %collective-permute-start) | collective-permute-done | bytes 524320 | tf_op jit(solution)/shard_map/while/body/eval_jaxpr/ppermute | solution.py:14
  264.6 10.7 %collective-permute-done = f32[8,128,128]{2,1,0:T(8,128)S(1)} collective-permute-done((f32[8,128,128]{2,1,0:T(8,128)S(1)}, f32[8,128,128]{2,1,0:T(8,128)S(1)}, u32[]{:S(2)}, u32[]{:S(2)}) %collective-permute-start) | collective-permute-done | bytes 524320 | tf_op jit(solution)/shard_map/while/body/eval_jaxpr/ppermute | solution.py:14
  277.3 10.7 %collective-permute-done = f32[8,128,128]{2,1,0:T(8,128)S(1)} collective-permute-done((f32[8,128,128]{2,1,0:T(8,128)S(1)}, f32[8,128,128]{2,1,0:T(8,128)S(1)}, u32[]{:S(2)}, u32[]{:S(2)}) %collective-permute-start) | collective-permute-done | bytes 524320 | tf_op jit(solution)/shard_map/while/body/eval_jaxpr/ppermute | solution.py:14
  290.0 10.7 %collective-permute-done = f32[8,128,128]{2,1,0:T(8,128)S(1)} collective-permute-done((f32[8,128,128]{2,1,0:T(8,128)S(1)}, f32[8,128,128]{2,1,0:T(8,128)S(1)}, u32[]{:S(2)}, u32[]{:S(2)}) %collective-permute-start) | collective-permute-done | bytes 524320 | tf_op jit(solution)/shard_map/while/body/eval_jaxpr/ppermute | solution.py:14
  302.6 10.7 %collective-permute-done = f32[8,128,128]{2,1,0:T(8,128)S(1)} collective-permute-done((f32[8,128,128]{2,1,0:T(8,128)S(1)}, f32[8,128,128]{2,1,0:T(8,128)S(1)}, u32[]{:S(2)}, u32[]{:S(2)}) %collective-permute-start) | collective-permute-done | bytes 524320 | tf_op jit(solution)/shard_map/while/body/eval_jaxpr/ppermute | solution.py:14
  315.3 10.7 %collective-permute-done = f32[8,128,128]{2,1,0:T(8,128)S(1)} collective-permute-done((f32[8,128,128]{2,1,0:T(8,128)S(1)}, f32[8,128,128]{2,1,0:T(8,128)S(1)}, u32[]{:S(2)}, u32[]{:S(2)}) %collective-permute-start) | collective-permute-done | bytes 524320 | tf_op jit(solution)/shard_map/while/body/eval_jaxpr/ppermute | solution.py:14
  328.0 10.7 %collective-permute-done = f32[8,128,128]{2,1,0:T(8,128)S(1)} collective-permute-done((f32[8,128,128]{2,1,0:T(8,128)S(1)}, f32[8,128,128]{2,1,0:T(8,128)S(1)}, u32[]{:S(2)}, u32[]{:S(2)}) %collective-permute-start) | collective-permute-done | bytes 524320 | tf_op jit(solution)/shard_map/while/body/eval_jaxpr/ppermute | solution.py:14
  340.7 10.7 %collective-permute-done = f32[8,128,128]{2,1,0:T(8,128)S(1)} collective-permute-done((f32[8,128,128]{2,1,0:T(8,128)S(1)}, f32[8,128,128]{2,1,0:T(8,128)S(1)}, u32[]{:S(2)}, u32[]{:S(2)}) %collective-permute-start) | collective-permute-done | bytes 524320 | tf_op jit(solution)/shard_map/while/body/eval_jaxpr/ppermute | solution.py:14
  353.3 10.7 %collective-permute-done = f32[8,128,128]{2,1,0:T(8,128)S(1)} collective-permute-done((f32[8,128,128]{2,1,0:T(8,128)S(1)}, f32[8,128,128]{2,1,0:T(8,128)S(1)}, u32[]{:S(2)}, u32[]{:S(2)}) %collective-permute-start) | collective-permute-done | bytes 524320 | tf_op jit(solution)/shard_map/while/body/eval_jaxpr/ppermute | solution.py:14
  366.0 10.7 %collective-permute-done = f32[8,128,128]{2,1,0:T(8,128)S(1)} collective-permute-done((f32[8,128,128]{2,1,0:T(8,128)S(1)}, f32[8,128,128]{2,1,0:T(8,128)S(1)}, u32[]{:S(2)}, u32[]{:S(2)}) %collective-permute-start) | collective-permute-done | bytes 524320 | tf_op jit(solution)/shard_map/while/body/eval_jaxpr/ppermute | solution.py:14
  378.7 10.7 %collective-permute-done = f32[8,128,128]{2,1,0:T(8,128)S(1)} collective-permute-done((f32[8,128,128]{2,1,0:T(8,128)S(1)}, f32[8,128,128]{2,1,0:T(8,128)S(1)}, u32[]{:S(2)}, u32[]{:S(2)}) %collective-permute-start) | collective-permute-done | bytes 524320 | tf_op jit(solution)/shard_map/while/body/eval_jaxpr/ppermute | solution.py:14
  391.3 10.7 %collective-permute-done = f32[8,128,128]{2,1,0:T(8,128)S(1)} collective-permute-done((f32[8,128,128]{2,1,0:T(8,128)S(1)}, f32[8,128,128]{2,1,0:T(8,128)S(1)}, u32[]{:S(2)}, u32[]{:S(2)}) %collective-permute-start) | collective-permute-done | bytes 524320 | tf_op jit(solution)/shard_map/while/body/eval_jaxpr/ppermute | solution.py:14
  404.0 10.7 %collective-permute-done = f32[8,128,128]{2,1,0:T(8,128)S(1)} collective-permute-done((f32[8,128,128]{2,1,0:T(8,128)S(1)}, f32[8,128,128]{2,1,0:T(8,128)S(1)}, u32[]{:S(2)}, u32[]{:S(2)}) %collective-permute-start) | collective-permute-done | bytes 524320 | tf_op jit(solution)/shard_map/while/body/eval_jaxpr/ppermute | solution.py:14
  416.7 10.7 %collective-permute-done = f32[8,128,128]{2,1,0:T(8,128)S(1)} collective-permute-done((f32[8,128,128]{2,1,0:T(8,128)S(1)}, f32[8,128,128]{2,1,0:T(8,128)S(1)}, u32[]{:S(2)}, u32[]{:S(2)}) %collective-permute-start) | collective-permute-done | bytes 524320 | tf_op jit(solution)/shard_map/while/body/eval_jaxpr/ppermute | solution.py:14
  429.3 10.7 %collective-permute-done = f32[8,128,128]{2,1,0:T(8,128)S(1)} collective-permute-done((f32[8,128,128]{2,1,0:T(8,128)S(1)}, f32[8,128,128]{2,1,0:T(8,128)S(1)}, u32[]{:S(2)}, u32[]{:S(2)}) %collective-permute-start) | collective-permute-done | bytes 524320 | tf_op jit(solution)/shard_map/while/body/eval_jaxpr/ppermute | solution.py:14
  442.0 10.7 %collective-permute-done = f32[8,128,128]{2,1,0:T(8,128)S(1)} collective-permute-done((f32[8,128,128]{2,1,0:T(8,128)S(1)}, f32[8,128,128]{2,1,0:T(8,128)S(1)}, u32[]{:S(2)}, u32[]{:S(2)}) %collective-permute-start) | collective-permute-done | bytes 524320 | tf_op jit(solution)/shard_map/while/body/eval_jaxpr/ppermute | solution.py:14
  454.7 10.7 %collective-permute-done = f32[8,128,128]{2,1,0:T(8,128)S(1)} collective-permute-done((f32[8,128,128]{2,1,0:T(8,128)S(1)}, f32[8,128,128]{2,1,0:T(8,128)S(1)}, u32[]{:S(2)}, u32[]{:S(2)}) %collective-permute-start) | collective-permute-done | bytes 524320 | tf_op jit(solution)/shard_map/while/body/eval_jaxpr/ppermute | solution.py:14
  467.4 10.7 %collective-permute-done = f32[8,128,128]{2,1,0:T(8,128)S(1)} collective-permute-done((f32[8,128,128]{2,1,0:T(8,128)S(1)}, f32[8,128,128]{2,1,0:T(8,128)S(1)}, u32[]{:S(2)}, u32[]{:S(2)}) %collective-permute-start) | collective-permute-done | bytes 524320 | tf_op jit(solution)/shard_map/while/body/eval_jaxpr/ppermute | solution.py:14
  480.0 10.7 %collective-permute-done = f32[8,128,128]{2,1,0:T(8,128)S(1)} collective-permute-done((f32[8,128,128]{2,1,0:T(8,128)S(1)}, f32[8,128,128]{2,1,0:T(8,128)S(1)}, u32[]{:S(2)}, u32[]{:S(2)}) %collective-permute-start) | collective-permute-done | bytes 524320 | tf_op jit(solution)/shard_map/while/body/eval_jaxpr/ppermute | solution.py:14
  553.9 49.4 %all_to_all.50 = bf16[1024,8,128]{2,1,0:T(8,128)(2,1)} all-to-all(bf16[1024,8,128]{2,1,0:T(8,128)(2,1)S(1)} %bitcast.74), channel_id=1, replica_groups=mesh['seq'=32,'head'=8] {'head'}, dimensions={0} | all-to-all | bytes 4194304 | tf_op jit(solution)/shard_map/all_to_all | solution.py:75
  (110 shorter events, 173.9 us)
Async XLA Ops:
  8.4 59.7 %all-to-all-start = ((bf16[8,128,8,128]{3,2,1,0:T(8,128)(2,1)}), bf16[8,128,8,128]{3,2,1,0:T(8,128)(2,1)S(1)}, u32[]{:S(2)}, u32[]{:S(2)}) async-start(bf16[8,128,8,128]{3,2,1,0:T(8,128)(2,1)} %fusion.20), calls=%async_computation | async-start | bytes 4194304 | tf_op jit(solution)/shard_map/all_to_all | solution.py:51
  68.0 56.0 %all-to-all-start.1 = ((bf16[128,64,128]{2,0,1:T(8,128)(2,1)}), bf16[128,64,128]{2,0,1:T(8,128)(2,1)}, u32[]{:S(2)}, u32[]{:S(2)}) async-start(bf16[128,64,128]{2,0,1:T(8,128)(2,1)} %copy.40), calls=%async_computation.1 | async-start | bytes 4194304 | tf_op jit(solution)/shard_map/all_to_all | solution.py:49
  124.0 405.7 %all-to-all-start.2 = ((bf16[128,64,128]{2,0,1:T(8,128)(2,1)}), bf16[128,64,128]{2,0,1:T(8,128)(2,1)}, u32[]{:S(2)}, u32[]{:S(2)}) async-start(bf16[128,64,128]{2,0,1:T(8,128)(2,1)} %copy.48), calls=%async_computation.2 | async-start | bytes 4194304 | tf_op jit(solution)/shard_map/all_to_all | solution.py:48
  136.0 12.6 %collective-permute-start = (f32[8,128,128]{2,1,0:T(8,128)S(1)}, f32[8,128,128]{2,1,0:T(8,128)S(1)}, u32[]{:S(2)}, u32[]{:S(2)}) collective-permute-start(f32[8,128,128]{2,1,0:T(8,128)S(1)} %add.47), channel_id=1, source_target_pairs={{0,8},{8,16},{16,24},{24,32},{32,40},{40,48},{48,56},{56,64},{64,7... | collective-permute-start | bytes 1572872 | tf_op jit(solution)/shard_map/while/body/eval_jaxpr/ppermute | solution.py:14
  148.7 12.6 %collective-permute-start = (f32[8,128,128]{2,1,0:T(8,128)S(1)}, f32[8,128,128]{2,1,0:T(8,128)S(1)}, u32[]{:S(2)}, u32[]{:S(2)}) collective-permute-start(f32[8,128,128]{2,1,0:T(8,128)S(1)} %add.47), channel_id=1, source_target_pairs={{0,8},{8,16},{16,24},{24,32},{32,40},{40,48},{48,56},{56,64},{64,7... | collective-permute-start | bytes 1572872 | tf_op jit(solution)/shard_map/while/body/eval_jaxpr/ppermute | solution.py:14
  161.3 12.6 %collective-permute-start = (f32[8,128,128]{2,1,0:T(8,128)S(1)}, f32[8,128,128]{2,1,0:T(8,128)S(1)}, u32[]{:S(2)}, u32[]{:S(2)}) collective-permute-start(f32[8,128,128]{2,1,0:T(8,128)S(1)} %add.47), channel_id=1, source_target_pairs={{0,8},{8,16},{16,24},{24,32},{32,40},{40,48},{48,56},{56,64},{64,7... | collective-permute-start | bytes 1572872 | tf_op jit(solution)/shard_map/while/body/eval_jaxpr/ppermute | solution.py:14
  174.0 12.6 %collective-permute-start = (f32[8,128,128]{2,1,0:T(8,128)S(1)}, f32[8,128,128]{2,1,0:T(8,128)S(1)}, u32[]{:S(2)}, u32[]{:S(2)}) collective-permute-start(f32[8,128,128]{2,1,0:T(8,128)S(1)} %add.47), channel_id=1, source_target_pairs={{0,8},{8,16},{16,24},{24,32},{32,40},{40,48},{48,56},{56,64},{64,7... | collective-permute-start | bytes 1572872 | tf_op jit(solution)/shard_map/while/body/eval_jaxpr/ppermute | solution.py:14
  186.7 12.6 %collective-permute-start = (f32[8,128,128]{2,1,0:T(8,128)S(1)}, f32[8,128,128]{2,1,0:T(8,128)S(1)}, u32[]{:S(2)}, u32[]{:S(2)}) collective-permute-start(f32[8,128,128]{2,1,0:T(8,128)S(1)} %add.47), channel_id=1, source_target_pairs={{0,8},{8,16},{16,24},{24,32},{32,40},{40,48},{48,56},{56,64},{64,7... | collective-permute-start | bytes 1572872 | tf_op jit(solution)/shard_map/while/body/eval_jaxpr/ppermute | solution.py:14
  199.4 12.6 %collective-permute-start = (f32[8,128,128]{2,1,0:T(8,128)S(1)}, f32[8,128,128]{2,1,0:T(8,128)S(1)}, u32[]{:S(2)}, u32[]{:S(2)}) collective-permute-start(f32[8,128,128]{2,1,0:T(8,128)S(1)} %add.47), channel_id=1, source_target_pairs={{0,8},{8,16},{16,24},{24,32},{32,40},{40,48},{48,56},{56,64},{64,7... | collective-permute-start | bytes 1572872 | tf_op jit(solution)/shard_map/while/body/eval_jaxpr/ppermute | solution.py:14
  212.0 12.6 %collective-permute-start = (f32[8,128,128]{2,1,0:T(8,128)S(1)}, f32[8,128,128]{2,1,0:T(8,128)S(1)}, u32[]{:S(2)}, u32[]{:S(2)}) collective-permute-start(f32[8,128,128]{2,1,0:T(8,128)S(1)} %add.47), channel_id=1, source_target_pairs={{0,8},{8,16},{16,24},{24,32},{32,40},{40,48},{48,56},{56,64},{64,7... | collective-permute-start | bytes 1572872 | tf_op jit(solution)/shard_map/while/body/eval_jaxpr/ppermute | solution.py:14
  224.7 12.6 %collective-permute-start = (f32[8,128,128]{2,1,0:T(8,128)S(1)}, f32[8,128,128]{2,1,0:T(8,128)S(1)}, u32[]{:S(2)}, u32[]{:S(2)}) collective-permute-start(f32[8,128,128]{2,1,0:T(8,128)S(1)} %add.47), channel_id=1, source_target_pairs={{0,8},{8,16},{16,24},{24,32},{32,40},{40,48},{48,56},{56,64},{64,7... | collective-permute-start | bytes 1572872 | tf_op jit(solution)/shard_map/while/body/eval_jaxpr/ppermute | solution.py:14
  237.4 12.6 %collective-permute-start = (f32[8,128,128]{2,1,0:T(8,128)S(1)}, f32[8,128,128]{2,1,0:T(8,128)S(1)}, u32[]{:S(2)}, u32[]{:S(2)}) collective-permute-start(f32[8,128,128]{2,1,0:T(8,128)S(1)} %add.47), channel_id=1, source_target_pairs={{0,8},{8,16},{16,24},{24,32},{32,40},{40,48},{48,56},{56,64},{64,7... | collective-permute-start | bytes 1572872 | tf_op jit(solution)/shard_map/while/body/eval_jaxpr/ppermute | solution.py:14
  250.0 12.6 %collective-permute-start = (f32[8,128,128]{2,1,0:T(8,128)S(1)}, f32[8,128,128]{2,1,0:T(8,128)S(1)}, u32[]{:S(2)}, u32[]{:S(2)}) collective-permute-start(f32[8,128,128]{2,1,0:T(8,128)S(1)} %add.47), channel_id=1, source_target_pairs={{0,8},{8,16},{16,24},{24,32},{32,40},{40,48},{48,56},{56,64},{64,7... | collective-permute-start | bytes 1572872 | tf_op jit(solution)/shard_map/while/body/eval_jaxpr/ppermute | solution.py:14
  262.7 12.6 %collective-permute-start = (f32[8,128,128]{2,1,0:T(8,128)S(1)}, f32[8,128,128]{2,1,0:T(8,128)S(1)}, u32[]{:S(2)}, u32[]{:S(2)}) collective-permute-start(f32[8,128,128]{2,1,0:T(8,128)S(1)} %add.47), channel_id=1, source_target_pairs={{0,8},{8,16},{16,24},{24,32},{32,40},{40,48},{48,56},{56,64},{64,7... | collective-permute-start | bytes 1572872 | tf_op jit(solution)/shard_map/while/body/eval_jaxpr/ppermute | solution.py:14
  275.4 12.6 %collective-permute-start = (f32[8,128,128]{2,1,0:T(8,128)S(1)}, f32[8,128,128]{2,1,0:T(8,128)S(1)}, u32[]{:S(2)}, u32[]{:S(2)}) collective-permute-start(f32[8,128,128]{2,1,0:T(8,128)S(1)} %add.47), channel_id=1, source_target_pairs={{0,8},{8,16},{16,24},{24,32},{32,40},{40,48},{48,56},{56,64},{64,7... | collective-permute-start | bytes 1572872 | tf_op jit(solution)/shard_map/while/body/eval_jaxpr/ppermute | solution.py:14
  288.0 12.6 %collective-permute-start = (f32[8,128,128]{2,1,0:T(8,128)S(1)}, f32[8,128,128]{2,1,0:T(8,128)S(1)}, u32[]{:S(2)}, u32[]{:S(2)}) collective-permute-start(f32[8,128,128]{2,1,0:T(8,128)S(1)} %add.47), channel_id=1, source_target_pairs={{0,8},{8,16},{16,24},{24,32},{32,40},{40,48},{48,56},{56,64},{64,7... | collective-permute-start | bytes 1572872 | tf_op jit(solution)/shard_map/while/body/eval_jaxpr/ppermute | solution.py:14
  300.7 12.6 %collective-permute-start = (f32[8,128,128]{2,1,0:T(8,128)S(1)}, f32[8,128,128]{2,1,0:T(8,128)S(1)}, u32[]{:S(2)}, u32[]{:S(2)}) collective-permute-start(f32[8,128,128]{2,1,0:T(8,128)S(1)} %add.47), channel_id=1, source_target_pairs={{0,8},{8,16},{16,24},{24,32},{32,40},{40,48},{48,56},{56,64},{64,7... | collective-permute-start | bytes 1572872 | tf_op jit(solution)/shard_map/while/body/eval_jaxpr/ppermute | solution.py:14
  313.4 12.6 %collective-permute-start = (f32[8,128,128]{2,1,0:T(8,128)S(1)}, f32[8,128,128]{2,1,0:T(8,128)S(1)}, u32[]{:S(2)}, u32[]{:S(2)}) collective-permute-start(f32[8,128,128]{2,1,0:T(8,128)S(1)} %add.47), channel_id=1, source_target_pairs={{0,8},{8,16},{16,24},{24,32},{32,40},{40,48},{48,56},{56,64},{64,7... | collective-permute-start | bytes 1572872 | tf_op jit(solution)/shard_map/while/body/eval_jaxpr/ppermute | solution.py:14
  326.1 12.6 %collective-permute-start = (f32[8,128,128]{2,1,0:T(8,128)S(1)}, f32[8,128,128]{2,1,0:T(8,128)S(1)}, u32[]{:S(2)}, u32[]{:S(2)}) collective-permute-start(f32[8,128,128]{2,1,0:T(8,128)S(1)} %add.47), channel_id=1, source_target_pairs={{0,8},{8,16},{16,24},{24,32},{32,40},{40,48},{48,56},{56,64},{64,7... | collective-permute-start | bytes 1572872 | tf_op jit(solution)/shard_map/while/body/eval_jaxpr/ppermute | solution.py:14
  338.7 12.6 %collective-permute-start = (f32[8,128,128]{2,1,0:T(8,128)S(1)}, f32[8,128,128]{2,1,0:T(8,128)S(1)}, u32[]{:S(2)}, u32[]{:S(2)}) collective-permute-start(f32[8,128,128]{2,1,0:T(8,128)S(1)} %add.47), channel_id=1, source_target_pairs={{0,8},{8,16},{16,24},{24,32},{32,40},{40,48},{48,56},{56,64},{64,7... | collective-permute-start | bytes 1572872 | tf_op jit(solution)/shard_map/while/body/eval_jaxpr/ppermute | solution.py:14
  351.4 12.6 %collective-permute-start = (f32[8,128,128]{2,1,0:T(8,128)S(1)}, f32[8,128,128]{2,1,0:T(8,128)S(1)}, u32[]{:S(2)}, u32[]{:S(2)}) collective-permute-start(f32[8,128,128]{2,1,0:T(8,128)S(1)} %add.47), channel_id=1, source_target_pairs={{0,8},{8,16},{16,24},{24,32},{32,40},{40,48},{48,56},{56,64},{64,7... | collective-permute-start | bytes 1572872 | tf_op jit(solution)/shard_map/while/body/eval_jaxpr/ppermute | solution.py:14
  364.1 12.6 %collective-permute-start = (f32[8,128,128]{2,1,0:T(8,128)S(1)}, f32[8,128,128]{2,1,0:T(8,128)S(1)}, u32[]{:S(2)}, u32[]{:S(2)}) collective-permute-start(f32[8,128,128]{2,1,0:T(8,128)S(1)} %add.47), channel_id=1, source_target_pairs={{0,8},{8,16},{16,24},{24,32},{32,40},{40,48},{48,56},{56,64},{64,7... | collective-permute-start | bytes 1572872 | tf_op jit(solution)/shard_map/while/body/eval_jaxpr/ppermute | solution.py:14
  376.7 12.6 %collective-permute-start = (f32[8,128,128]{2,1,0:T(8,128)S(1)}, f32[8,128,128]{2,1,0:T(8,128)S(1)}, u32[]{:S(2)}, u32[]{:S(2)}) collective-permute-start(f32[8,128,128]{2,1,0:T(8,128)S(1)} %add.47), channel_id=1, source_target_pairs={{0,8},{8,16},{16,24},{24,32},{32,40},{40,48},{48,56},{56,64},{64,7... | collective-permute-start | bytes 1572872 | tf_op jit(solution)/shard_map/while/body/eval_jaxpr/ppermute | solution.py:14
  389.4 12.6 %collective-permute-start = (f32[8,128,128]{2,1,0:T(8,128)S(1)}, f32[8,128,128]{2,1,0:T(8,128)S(1)}, u32[]{:S(2)}, u32[]{:S(2)}) collective-permute-start(f32[8,128,128]{2,1,0:T(8,128)S(1)} %add.47), channel_id=1, source_target_pairs={{0,8},{8,16},{16,24},{24,32},{32,40},{40,48},{48,56},{56,64},{64,7... | collective-permute-start | bytes 1572872 | tf_op jit(solution)/shard_map/while/body/eval_jaxpr/ppermute | solution.py:14
  402.1 12.6 %collective-permute-start = (f32[8,128,128]{2,1,0:T(8,128)S(1)}, f32[8,128,128]{2,1,0:T(8,128)S(1)}, u32[]{:S(2)}, u32[]{:S(2)}) collective-permute-start(f32[8,128,128]{2,1,0:T(8,128)S(1)} %add.47), channel_id=1, source_target_pairs={{0,8},{8,16},{16,24},{24,32},{32,40},{40,48},{48,56},{56,64},{64,7... | collective-permute-start | bytes 1572872 | tf_op jit(solution)/shard_map/while/body/eval_jaxpr/ppermute | solution.py:14
  414.7 12.6 %collective-permute-start = (f32[8,128,128]{2,1,0:T(8,128)S(1)}, f32[8,128,128]{2,1,0:T(8,128)S(1)}, u32[]{:S(2)}, u32[]{:S(2)}) collective-permute-start(f32[8,128,128]{2,1,0:T(8,128)S(1)} %add.47), channel_id=1, source_target_pairs={{0,8},{8,16},{16,24},{24,32},{32,40},{40,48},{48,56},{56,64},{64,7... | collective-permute-start | bytes 1572872 | tf_op jit(solution)/shard_map/while/body/eval_jaxpr/ppermute | solution.py:14
  427.4 12.6 %collective-permute-start = (f32[8,128,128]{2,1,0:T(8,128)S(1)}, f32[8,128,128]{2,1,0:T(8,128)S(1)}, u32[]{:S(2)}, u32[]{:S(2)}) collective-permute-start(f32[8,128,128]{2,1,0:T(8,128)S(1)} %add.47), channel_id=1, source_target_pairs={{0,8},{8,16},{16,24},{24,32},{32,40},{40,48},{48,56},{56,64},{64,7... | collective-permute-start | bytes 1572872 | tf_op jit(solution)/shard_map/while/body/eval_jaxpr/ppermute | solution.py:14
  440.1 12.6 %collective-permute-start = (f32[8,128,128]{2,1,0:T(8,128)S(1)}, f32[8,128,128]{2,1,0:T(8,128)S(1)}, u32[]{:S(2)}, u32[]{:S(2)}) collective-permute-start(f32[8,128,128]{2,1,0:T(8,128)S(1)} %add.47), channel_id=1, source_target_pairs={{0,8},{8,16},{16,24},{24,32},{32,40},{40,48},{48,56},{56,64},{64,7... | collective-permute-start | bytes 1572872 | tf_op jit(solution)/shard_map/while/body/eval_jaxpr/ppermute | solution.py:14
  452.8 12.6 %collective-permute-start = (f32[8,128,128]{2,1,0:T(8,128)S(1)}, f32[8,128,128]{2,1,0:T(8,128)S(1)}, u32[]{:S(2)}, u32[]{:S(2)}) collective-permute-start(f32[8,128,128]{2,1,0:T(8,128)S(1)} %add.47), channel_id=1, source_target_pairs={{0,8},{8,16},{16,24},{24,32},{32,40},{40,48},{48,56},{56,64},{64,7... | collective-permute-start | bytes 1572872 | tf_op jit(solution)/shard_map/while/body/eval_jaxpr/ppermute | solution.py:14
  465.4 12.6 %collective-permute-start = (f32[8,128,128]{2,1,0:T(8,128)S(1)}, f32[8,128,128]{2,1,0:T(8,128)S(1)}, u32[]{:S(2)}, u32[]{:S(2)}) collective-permute-start(f32[8,128,128]{2,1,0:T(8,128)S(1)} %add.47), channel_id=1, source_target_pairs={{0,8},{8,16},{16,24},{24,32},{32,40},{40,48},{48,56},{56,64},{64,7... | collective-permute-start | bytes 1572872 | tf_op jit(solution)/shard_map/while/body/eval_jaxpr/ppermute | solution.py:14
  478.1 12.6 %collective-permute-start = (f32[8,128,128]{2,1,0:T(8,128)S(1)}, f32[8,128,128]{2,1,0:T(8,128)S(1)}, u32[]{:S(2)}, u32[]{:S(2)}) collective-permute-start(f32[8,128,128]{2,1,0:T(8,128)S(1)} %add.47), channel_id=1, source_target_pairs={{0,8},{8,16},{16,24},{24,32},{32,40},{40,48},{48,56},{56,64},{64,7... | collective-permute-start | bytes 1572872 | tf_op jit(solution)/shard_map/while/body/eval_jaxpr/ppermute | solution.py:14
  490.8 12.6 %collective-permute-start = (f32[8,128,128]{2,1,0:T(8,128)S(1)}, f32[8,128,128]{2,1,0:T(8,128)S(1)}, u32[]{:S(2)}, u32[]{:S(2)}) collective-permute-start(f32[8,128,128]{2,1,0:T(8,128)S(1)} %add.47), channel_id=1, source_target_pairs={{0,8},{8,16},{16,24},{24,32},{32,40},{40,48},{48,56},{56,64},{64,7... | collective-permute-start | bytes 1572872 | tf_op jit(solution)/shard_map/while/body/eval_jaxpr/ppermute | solution.py:14
  (8 other events, 48.9 us)
